TPU v7x, 32 devices: a whole 2x2x4 slice. The times are simulated.
32 devices in a mesh: row: 16 (over z, y, x), tok: 2 (over core).
Axes of the slice: x: 2, y: 2, z: 4, core: 2. Of those that a mesh axis runs over, the one named last changes fastest.
Arguments:
- tokens: bfloat16 [16, 512, 768], P('row', 'tok'), may hold values from -6 to 6
- cotangent: bfloat16 [16, 512, 768], P('row', 'tok'), may hold values from -6 to 6
- segment_ids: int32 [16, 512], P('row', 'tok'), may hold values from 0 to 5, never falling along the last dimension, each value on 1 to 256 neighbouring positions
- valid: int32 [16, 512], P('row', 'tok'), may hold values from 0 to 1, as said below
- first_gain: float32 [2, 768], replicated, may hold values from 0.5 to 1.5
- first_shift: float32 [2, 768], replicated, may hold values from -2 to 2
- joint_weight: bfloat16 [2, 768, 2304], replicated, may hold values from -0.21875 to 0.21875
- joint_bias: float32 [2, 2, 768], replicated, may hold values from -2 to 2
- output_weight: bfloat16 [2, 768, 768], replicated, may hold values from -1.25 to 1.25
- output_bias: float32 [2, 768], replicated, may hold values from -2 to 2
- second_gain: float32 [2, 768], replicated, may hold values from 0.5 to 1.5
- second_shift: float32 [2, 768], replicated, may hold values from -2 to 2
- up_weight: bfloat16 [2, 768, 3072], replicated, may hold values from -0.21875 to 0.21875
- up_bias: float32 [2, 3072], replicated, may hold values from -2 to 2
- down_weight: bfloat16 [2, 3072, 768], replicated, may hold values from -0.109375 to 0.109375
- down_bias: float32 [2, 768], replicated, may hold values from -2 to 2
Outputs:
- output: bfloat16 [16, 512, 768], P('row', 'tok')
- input_gradient: float32 [16, 512, 768], P('row', 'tok')
- first_gain_gradient: float32 [2, 768], P(None, ('row', 'tok'))
- first_shift_gradient: float32 [2, 768], P(None, ('row', 'tok'))
- joint_weight_gradient: float32 [2, 768, 2304], P(None, ('row', 'tok'))
- joint_bias_gradient: float32 [2, 2, 768], P(None, None, ('row', 'tok'))
- output_weight_gradient: float32 [2, 768, 768], P(None, ('row', 'tok'))
- output_bias_gradient: float32 [2, 768], P(None, ('row', 'tok'))
- second_gain_gradient: float32 [2, 768], P(None, ('row', 'tok'))
- second_shift_gradient: float32 [2, 768], P(None, ('row', 'tok'))
- up_weight_gradient: float32 [2, 768, 3072], P(None, ('row', 'tok'))
- up_bias_gradient: float32 [2, 3072], P(None, ('row', 'tok'))
- down_weight_gradient: float32 [2, 3072, 768], P(None, ('row', 'tok'))
- down_bias_gradient: float32 [2, 768], P(None, ('row', 'tok'))
Inputs may be any that keep to these rules, and one draw needn't show every extreme that they name: `valid`: in every row the ones come first and the zeros, at most 64 of them, fill its end.
All inputs are finite; a program needn't handle non-finite values.
Results may differ from a plain program's by a relative error of at most 0.014.
Values may be sent and summed in bfloat16 or wider, within the bound.
No kernel may reach another device: no remote copies, remote signals or barrier semaphores. Data moves between devices by JAX's collectives and lax.ppermute only.
A program may use at most 320 MiB of HBM per device.

v0:
```python
import jax
import jax.numpy as jnp
from jax import lax
from jax.sharding import PartitionSpec as P

epsilon = 1e-05
score_scale = 0.125
masked_score = -1e30


def normalize(stream):
    centre = stream - jnp.mean(stream, axis=-1, keepdims=True)
    inverse = lax.rsqrt(jnp.mean(centre * centre, axis=-1, keepdims=True) + epsilon)
    return (centre * inverse, inverse)


def norm_back(upstream, unit, inverse, gain):
    scaled = upstream * gain
    return inverse * (
        scaled
        - jnp.mean(scaled, axis=-1, keepdims=True)
        - unit * jnp.mean(scaled * unit, axis=-1, keepdims=True)
    )


def gelu_exact(preact):
    return jax.nn.gelu(preact, approximate=False)


def blocked(array, block_size):
    return array.reshape((array.shape[0] // block_size, block_size) + array.shape[1:])


def row_scores(queries, key_rows, code_block, code_all):
    scores = (
        jnp.einsum("qhd,khd->hqk", queries, key_rows, preferred_element_type=jnp.float32)
        * score_scale
    )
    allowed = code_block[:, None] == code_all[None, :]
    return jnp.where(allowed[None], scores, masked_score)


def attention(queries, key_rows, value_rows, code_local, code_all):
    block_size = min(512, queries.shape[0])

    def one_block(pieces):
        scores = row_scores(pieces[0], key_rows, pieces[1], code_all)
        row_max = jnp.max(scores, axis=-1, keepdims=True)
        exponent = jnp.exp(scores - row_max)
        totals = jnp.sum(exponent, axis=-1, keepdims=True)
        soft_low = (exponent / totals).astype(jnp.bfloat16)
        attended = jnp.einsum(
            "hqk,khd->qhd", soft_low, value_rows, preferred_element_type=jnp.float32
        )
        return (attended, (row_max + jnp.log(totals))[..., 0])

    attended, log_totals = lax.map(
        one_block, (blocked(queries, block_size), blocked(code_local, block_size))
    )
    rows = queries.shape[0]
    return (attended.reshape(rows, -1), log_totals)


def attention_back(queries, key_rows, value_rows, code_local, code_all, log_totals, attended_grad):
    block_size = min(512, queries.shape[0])

    def one_block(carry, pieces):
        key_grad, value_grad = carry
        query_block, code_block, log_block, grad_block = pieces
        scores = row_scores(query_block, key_rows, code_block, code_all)
        soft = jnp.exp(scores - log_block[..., None])
        soft_low = soft.astype(jnp.bfloat16)
        soft_grad = jnp.einsum(
            "qhd,khd->hqk", grad_block, value_rows, preferred_element_type=jnp.float32
        )
        delta = jnp.sum(soft_grad * soft, axis=-1, keepdims=True)
        score_grad = (soft * (soft_grad - delta)).astype(jnp.bfloat16)
        query_grad = (
            jnp.einsum("hqk,khd->qhd", score_grad, key_rows, preferred_element_type=jnp.float32)
            * score_scale
        )
        key_grad = (
            key_grad
            + jnp.einsum(
                "hqk,qhd->khd", score_grad, query_block, preferred_element_type=jnp.float32
            )
            * score_scale
        )
        value_grad = value_grad + jnp.einsum(
            "hqk,qhd->khd", soft_low, grad_block, preferred_element_type=jnp.float32
        )
        return ((key_grad, value_grad), query_grad)

    zeros = jnp.zeros(key_rows.shape, jnp.float32)
    (key_grad, value_grad), query_grad = lax.scan(
        one_block,
        (zeros, zeros),
        (
            blocked(queries, block_size),
            blocked(code_local, block_size),
            log_totals,
            blocked(attended_grad, block_size),
        ),
    )
    return (query_grad.reshape(queries.shape), key_grad, value_grad)


def project(stream, weight_set, heads):
    first_gain, first_shift, joint_weight, joint_bias = weight_set[:4]
    width = stream.shape[1]
    rows = stream.shape[0]
    unit_one, inverse_one = normalize(stream)
    normed_one = (unit_one * first_gain + first_shift).astype(jnp.bfloat16)
    mixed = jnp.dot(normed_one, joint_weight, preferred_element_type=jnp.float32)
    queries = (mixed[:, :width] + joint_bias[0]).astype(jnp.bfloat16).reshape(rows, heads, -1)
    key_rows = mixed[:, width : 2 * width].astype(jnp.bfloat16).reshape(rows, heads, -1)
    value_rows = (
        (mixed[:, 2 * width :] + joint_bias[1]).astype(jnp.bfloat16).reshape(rows, heads, -1)
    )
    return (unit_one, inverse_one, normed_one, queries, key_rows, value_rows)


def finish(stream, attended, weight_set):
    (
        output_weight,
        output_bias,
        second_gain,
        second_shift,
        up_weight,
        up_bias,
        down_weight,
        down_bias,
    ) = weight_set[4:]
    attended_low = attended.astype(jnp.bfloat16)
    middle = (
        stream
        + jnp.dot(attended_low, output_weight, preferred_element_type=jnp.float32)
        + output_bias
    )
    unit_two, inverse_two = normalize(middle)
    normed_two = (unit_two * second_gain + second_shift).astype(jnp.bfloat16)
    preact = jnp.dot(normed_two, up_weight, preferred_element_type=jnp.float32) + up_bias
    hidden = gelu_exact(preact).astype(jnp.bfloat16)
    result = middle + jnp.dot(hidden, down_weight, preferred_element_type=jnp.float32) + down_bias
    return (attended_low, middle, unit_two, inverse_two, normed_two, preact, hidden, result)


def left_product(left, right):
    return jnp.einsum("ti,tj->ij", left, right, preferred_element_type=jnp.float32)


def right_product(left, right):
    return jnp.einsum("tj,ij->ti", left, right, preferred_element_type=jnp.float32)


def body(
    tokens,
    cotangent,
    segment_ids,
    valid,
    first_gain,
    first_shift,
    joint_weight,
    joint_bias,
    output_weight,
    output_bias,
    second_gain,
    second_shift,
    up_weight,
    up_bias,
    down_weight,
    down_bias,
):
    params = (
        first_gain,
        first_shift,
        joint_weight,
        joint_bias,
        output_weight,
        output_bias,
        second_gain,
        second_shift,
        up_weight,
        up_bias,
        down_weight,
        down_bias,
    )
    layers = joint_weight.shape[0]
    width = joint_weight.shape[1]
    heads = width // 64
    rows = tokens.shape[1]
    code_local = segment_ids[0] * 2 + valid[0]
    code_all = lax.all_gather(code_local, "tok", axis=0, tiled=True)
    stream = tokens[0].astype(jnp.float32)
    saved = []
    kept = []
    for layer_index in range(layers):
        weight_set = tuple((member[layer_index] for member in params))
        saved.append(stream)
        unit_one, inverse_one, normed_one, queries, key_rows, value_rows = project(
            stream, weight_set, heads
        )
        key_all, value_all = (
            lax.all_gather(key_rows, "tok", axis=0, tiled=True),
            lax.all_gather(value_rows, "tok", axis=0, tiled=True),
        )
        kept.append((key_all, value_all))
        attended, log_totals = attention(queries, key_all, value_all, code_local, code_all)
        stream = finish(stream, attended, weight_set)[-1]
    output = stream.astype(jnp.bfloat16)[None]
    upstream = cotangent[0].astype(jnp.float32)
    gradients = [None] * layers
    for layer_index in reversed(range(layers)):
        weight_set = tuple((member[layer_index] for member in params))
        stream = saved[layer_index]
        unit_one, inverse_one, normed_one, queries, key_rows, value_rows = project(
            stream, weight_set, heads
        )
        key_all, value_all = (
            lax.all_gather(key_rows, "tok", axis=0, tiled=True),
            lax.all_gather(value_rows, "tok", axis=0, tiled=True),
        )
        attended, log_totals = attention(queries, key_all, value_all, code_local, code_all)
        attended_low, middle, unit_two, inverse_two, normed_two, preact, hidden, result = finish(
            stream, attended, weight_set
        )
        up_low = upstream.astype(jnp.bfloat16)
        down_bias_grad = jnp.sum(upstream, axis=0)
        down_weight_grad = left_product(hidden, up_low)
        hidden_grad = right_product(up_low, weight_set[10])
        gelu_pull = jax.vjp(gelu_exact, preact)[1]
        preact_grad = gelu_pull(hidden_grad)[0]
        up_bias_grad = jnp.sum(preact_grad, axis=0)
        preact_low = preact_grad.astype(jnp.bfloat16)
        up_weight_grad = left_product(normed_two, preact_low)
        normed_two_grad = right_product(preact_low, weight_set[8])
        second_gain_grad = jnp.sum(normed_two_grad * unit_two, axis=0)
        second_shift_grad = jnp.sum(normed_two_grad, axis=0)
        middle_grad = upstream + norm_back(normed_two_grad, unit_two, inverse_two, weight_set[6])
        middle_low = middle_grad.astype(jnp.bfloat16)
        output_bias_grad = jnp.sum(middle_grad, axis=0)
        output_weight_grad = left_product(attended_low, middle_low)
        attended_grad = (
            right_product(middle_low, weight_set[4]).astype(jnp.bfloat16).reshape(rows, heads, -1)
        )
        query_grad, key_grad_all, value_grad_all = attention_back(
            queries, key_all, value_all, code_local, code_all, log_totals, attended_grad
        )
        key_grad, value_grad = (
            lax.psum_scatter(
                key_grad_all.astype(jnp.bfloat16), "tok", scatter_dimension=0, tiled=True
            ).astype(jnp.float32),
            lax.psum_scatter(
                value_grad_all.astype(jnp.bfloat16), "tok", scatter_dimension=0, tiled=True
            ).astype(jnp.float32),
        )
        query_grad = query_grad.reshape(rows, width)
        key_grad = key_grad.reshape(rows, width)
        value_grad = value_grad.reshape(rows, width)
        joint_bias_grad = jnp.stack([jnp.sum(query_grad, axis=0), jnp.sum(value_grad, axis=0)])
        mixed_low = jnp.concatenate([query_grad, key_grad, value_grad], axis=1).astype(jnp.bfloat16)
        joint_weight_grad = left_product(normed_one, mixed_low)
        normed_one_grad = right_product(mixed_low, weight_set[2])
        first_gain_grad = jnp.sum(normed_one_grad * unit_one, axis=0)
        first_shift_grad = jnp.sum(normed_one_grad, axis=0)
        upstream = middle_grad + norm_back(normed_one_grad, unit_one, inverse_one, weight_set[0])
        gradients[layer_index] = (
            first_gain_grad,
            first_shift_grad,
            joint_weight_grad,
            joint_bias_grad,
            output_weight_grad,
            output_bias_grad,
            second_gain_grad,
            second_shift_grad,
            up_weight_grad,
            up_bias_grad,
            down_weight_grad,
            down_bias_grad,
        )
    stacked = [
        jnp.stack([gradients[layer_index][position] for layer_index in range(layers)])
        for position in range(12)
    ]
    summed = (
        lax.psum_scatter(stacked[0], ("row", "tok"), scatter_dimension=1, tiled=True),
        lax.psum_scatter(stacked[1], ("row", "tok"), scatter_dimension=1, tiled=True),
        lax.psum_scatter(stacked[2], ("row", "tok"), scatter_dimension=1, tiled=True),
        lax.psum_scatter(stacked[3], ("row", "tok"), scatter_dimension=2, tiled=True),
        lax.psum_scatter(stacked[4], ("row", "tok"), scatter_dimension=1, tiled=True),
        lax.psum_scatter(stacked[5], ("row", "tok"), scatter_dimension=1, tiled=True),
        lax.psum_scatter(stacked[6], ("row", "tok"), scatter_dimension=1, tiled=True),
        lax.psum_scatter(stacked[7], ("row", "tok"), scatter_dimension=1, tiled=True),
        lax.psum_scatter(stacked[8], ("row", "tok"), scatter_dimension=1, tiled=True),
        lax.psum_scatter(stacked[9], ("row", "tok"), scatter_dimension=1, tiled=True),
        lax.psum_scatter(stacked[10], ("row", "tok"), scatter_dimension=1, tiled=True),
        lax.psum_scatter(stacked[11], ("row", "tok"), scatter_dimension=1, tiled=True),
    )
    return (
        output,
        upstream[None],
        summed[0],
        summed[1],
        summed[2],
        summed[3],
        summed[4],
        summed[5],
        summed[6],
        summed[7],
        summed[8],
        summed[9],
        summed[10],
        summed[11],
    )


def solution(mesh):
    in_specs = (
        P("row", "tok", None),
        P("row", "tok", None),
        P("row", "tok"),
        P("row", "tok"),
        P(),
        P(),
        P(),
        P(),
        P(),
        P(),
        P(),
        P(),
        P(),
        P(),
        P(),
        P(),
    )
    out_specs = (
        P("row", "tok", None),
        P("row", "tok", None),
        P(None, ("row", "tok")),
        P(None, ("row", "tok")),
        P(None, ("row", "tok"), None),
        P(None, None, ("row", "tok")),
        P(None, ("row", "tok"), None),
        P(None, ("row", "tok")),
        P(None, ("row", "tok")),
        P(None, ("row", "tok")),
        P(None, ("row", "tok"), None),
        P(None, ("row", "tok")),
        P(None, ("row", "tok"), None),
        P(None, ("row", "tok")),
    )
    return jax.shard_map(body, mesh=mesh, in_specs=in_specs, out_specs=out_specs, check_vma=False)
```

profile of v0, /device:TPU:0, one launch (start us, length us, event | category | flops | bytes accessed | tf_op | source)
XLA Modules:
  0.0 974.1 jit_solution(4428300963790673774)
XLA Ops:
  18.1 3.3 fusion.40
  24.5 2.9 all_gather.19
  36.3 10.1 %multiply_convert_fusion.3 = (bf16[256,3072]{1,0:T(8,128)(2,1)S(1)}, f32[256,3072]{1,0:T(8,128)}, f32[256,3072]{1,0:T(8,128)}) fusion(f32[3072]{0:T(1024)S(1)} %bitcast.275, bf16[2,768,3072]{2,1,0:T(8,128)(2,1)S(1)} %bitcast.279, f32[256,768]{1,0:T(8,128)S(1)} %get-tuple-element.233, f32[768]{0:T(1024)S(1)} %get-tuple-element.173, ...), kind=kOutput, calls=%fused_computation.83 | convolution fusion | flops 1260847104 | bytes 13391872 | tf_op jit(solution)/shard_map/dot_general | solution.py:142
  68.5 9.8 %multiply_convert_fusion.2 = (bf16[256,3072]{1,0:T(8,128)(2,1)}, f32[256,3072]{1,0:T(8,128)S(1)}, f32[256,3072]{1,0:T(8,128)}) fusion(f32[3072]{0:T(1024)S(1)} %bitcast.273, bf16[2,768,3072]{2,1,0:T(8,128)(2,1)S(1)} %bitcast.281, f32[256,768]{1,0:T(8,128)S(1)} %get-tuple-element.240, f32[768]{0:T(1024)S(1)} %copy-done.62, f32[768]{0:T(1024)S(1)} %copy-done.53, ...), kind=kOutput, calls=%fused_computation.70 | convolution fusion | flops 1260847104 | bytes 13391872 | tf_op jit(solution)/shard_map/dot_general | solution.py:142
  78.3 4.4 fusion.180
  87.5 4.9 fusion.79
  92.7 3.9 multiply_reduce_fusion.1
  96.6 3.7 multiply_convert_fusion.1
  102.7 3.6 fusion.173
  106.3 8.9 reduce-scatter.19.cloned.1.call-done
  115.2 4.6 multiply_reduce_fusion.4
  121.7 5.5 fusion.181
  132.1 4.9 fusion.76
  137.1 3.9 multiply_reduce_fusion
  141.0 3.7 multiply_convert_fusion
  146.8 3.1 convolution_bitcast_fusion.6
  153.0 3.1 convolution_bitcast_fusion.7
  156.2 4.9 pad_maximum_fusion.3
  161.8 5.7 convolution_bitcast_fusion.4
  170.0 5.5 convolution_bitcast_fusion.5
  175.5 11.1 %pad_maximum_fusion.2 = f32[2,768,2304]{2,1,0:T(8,128)} fusion(f32[1,768,2304]{2,1,0:T(8,128)} %convolution_bitcast_fusion.4, f32[1,768,2304]{2,1,0:T(8,128)} %convolution_bitcast_fusion.5), kind=kLoop, calls=%fused_computation.2 | loop fusion | flops 3538944 | bytes 28311552 | tf_op jit(solution)/shard_map/stack | solution.py:282
  192.4 7.0 pad_maximum_fusion
  200.4 3.0 convolution_bitcast_fusion
  204.9 6.9 pad_maximum_fusion.1
  215.5 4.6 fusion.105
  227.9 33.6 %reduce-scatter.35.cloned.1.call-done = f32[96,2]{1,0:T(8,128)} async-done(((f32[3072,2]{1,0:T(8,128)}), f32[96,2]{1,0:T(8,128)}) %reduce-scatter.35.cloned.1.call-update) | async-done | bytes 784
  264.2 3.7 fusion.128
  268.0 41.0 %all-reduce.7 = (f32[2,768]{1,0:T(2,128)S(1)}, f32[2,768]{1,0:T(2,128)S(1)}, f32[2,2,768]{2,1,0:T(2,128)S(1)}, f32[2,768]{1,0:T(2,128)S(1)}, f32[2,768]{1,0:T(2,...) all-reduce(f32[2,768]{1,0:T(2,128)S(1)} %pad_maximum_fusion.12, ...), channel_id=7, replica_groups=mesh['row'=16,'tok'=2] {'row','tok'}, use_global_device_ids=true, to_apply=%region_28.29.clone | all-reduce | flops 12288 | bytes 98304
  314.6 58.9 %reduce-scatter.29.cloned.1.call-done = f32[2,24,768]{2,1,0:T(8,128)} async-done(((f32[2,768,768]{2,1,0:T(8,128)}), f32[2,24,768]{2,1,0:T(8,128)}) %reduce-scatter.29.cloned.1.call-update) | async-done | bytes 147472 | tf_op jit(solution)/shard_map/reduce_scatter | solution.py:290
  373.5 169.5 %reduce-scatter.27.cloned.1.call-done = f32[2,24,2304]{2,1,0:T(8,128)} async-done(((f32[2,768,2304]{2,1,0:T(8,128)}), f32[2,24,2304]{2,1,0:T(8,128)}) %reduce-scatter.27.cloned.1.call-update) | async-done | bytes 442384 | tf_op jit(solution)/shard_map/reduce_scatter | solution.py:288
  543.1 212.1 %reduce-scatter.31.cloned.1.call-done = f32[2,24,3072]{2,1,0:T(8,128)} async-done(((f32[2,768,3072]{2,1,0:T(8,128)}), f32[2,24,3072]{2,1,0:T(8,128)}) %reduce-scatter.31.cloned.1.call-update) | async-done | bytes 589840 | tf_op jit(solution)/shard_map/reduce_scatter | solution.py:294
  755.2 212.2 %reduce-scatter.33.cloned.1.call-done = f32[2,96,768]{2,1,0:T(8,128)} async-done(((f32[2,3072,768]{2,1,0:T(8,128)}), f32[2,96,768]{2,1,0:T(8,128)}) %reduce-scatter.33.cloned.1.call-update) | async-done | bytes 589840 | tf_op jit(solution)/shard_map/reduce_scatter | solution.py:296
  (365 shorter events, 94.7 us)
Async XLA Ops:
  7.2 99.1 %reduce-scatter.21.cloned.1.call-start = ((), (), s32[]{:S(2)}) async-start(), calls=%async_computation.10 | async-start | bytes 1179648 | tf_op jit(solution)/shard_map/reduce_scatter | solution.py:253
  8.4 13.0 %copy-start.66 = (f32[256]{0:T(256)}, f32[256]{0:T(256)S(1)}, u32[]{:S(2)}) copy-start(f32[256]{0:T(256)S(1)} %broadcast_multiply_fusion.11) | copy-start | bytes 3076
  9.6 11.8 %copy-start.79 = (f32[256]{0:T(256)}, f32[256]{0:T(256)S(1)}, u32[]{:S(2)}) copy-start(f32[256]{0:T(256)S(1)} %add_rsqrt_fusion.3) | copy-start | bytes 3076
  18.1 30.2 %copy-start.47 = (f32[768]{0:T(1024)}, f32[768]{0:T(1024)S(1)}, u32[]{:S(2)}) copy-start(f32[768]{0:T(1024)S(1)} %get-tuple-element.257) | copy-start | bytes 9220
  18.1 30.2 %copy-start.58 = (f32[768]{0:T(1024)}, f32[768]{0:T(1024)S(1)}, u32[]{:S(2)}) copy-start(f32[768]{0:T(1024)S(1)} %get-tuple-element.189) | copy-start | bytes 9220
  34.4 12.0 %slice-start.9 = ((s8[9437184]{0:T(1024)(128)(4,1)}), s8[4194304]{0:T(1024)(128)(4,1)S(1)}, s32[]{:S(2)}) async-start(s8[9437184]{0:T(1024)(128)(4,1)} %bitcast.284), calls=%async_computation.27 | async-start | bytes 8388608
  34.4 13.9 %slice-start.15 = ((s8[7077888]{0:T(1024)(128)(4,1)}), s8[4194304]{0:T(1024)(128)(4,1)S(1)}, s32[]{:S(2)}) async-start(s8[7077888]{0:T(1024)(128)(4,1)} %bitcast.288), calls=%async_computation.33 | async-start | bytes 8388608
  35.0 11.4 %copy-start.15 = (f32[256,768]{1,0:T(8,128)}, f32[256,768]{1,0:T(8,128)S(1)}, u32[]{:S(2)}) copy-start(f32[256,768]{1,0:T(8,128)S(1)} %get-tuple-element.233) | copy-start | bytes 2359300
  35.0 11.4 %copy-start.69 = (f32[256]{0:T(256)}, f32[256]{0:T(256)S(1)}, u32[]{:S(2)}) copy-start(f32[256]{0:T(256)S(1)} %broadcast_multiply_fusion.10) | copy-start | bytes 3076
  35.6 10.8 %copy-start.82 = (f32[256]{0:T(256)}, f32[256]{0:T(256)S(1)}, u32[]{:S(2)}) copy-start(f32[256]{0:T(256)S(1)} %add_rsqrt_fusion.2) | copy-start | bytes 3076
  36.3 10.1 %copy-start.60 = (f32[768]{0:T(1024)}, f32[768]{0:T(1024)S(1)}, u32[]{:S(2)}) copy-start(f32[768]{0:T(1024)S(1)} %get-tuple-element.173) | copy-start | bytes 9220
  36.3 10.1 %slice-start.10 = ((s8[9437184]{0:T(1024)(128)(4,1)}), s8[4194304]{0:T(1024)(128)(4,1)S(1)}, s32[]{:S(2)}) async-start(s8[9437184]{0:T(1024)(128)(4,1)} %bitcast.284), calls=%async_computation.28 | async-start | bytes 8388608
  36.3 12.0 %slice-start.16 = ((s8[7077888]{0:T(1024)(128)(4,1)}), s8[2883584]{0:T(1024)(128)(4,1)S(1)}, s32[]{:S(2)}) async-start(s8[7077888]{0:T(1024)(128)(4,1)} %bitcast.288), calls=%async_computation.34 | async-start | bytes 5767168
  48.0 18.4 %copy-start.8 = (f32[256,768]{1,0:T(8,128)}, f32[256,768]{1,0:T(8,128)S(1)}, u32[]{:S(2)}) copy-start(f32[256,768]{1,0:T(8,128)S(1)} %get-tuple-element.236) | copy-start | bytes 2359300
  66.3 12.0 %copy-start.36 = (bf16[12,64,256]{2,1,0:T(8,128)(2,1)}, bf16[12,64,256]{2,1,0:T(8,128)(2,1)S(1)}, u32[]{:S(2)}) copy-start(bf16[12,64,256]{2,1,0:T(8,128)(2,1)S(1)} %fusion.103) | copy-start | bytes 1179652
  66.5 11.8 %slice-start.12 = ((s8[9437184]{0:T(1024)(128)(4,1)}), s8[4194304]{0:T(1024)(128)(4,1)S(1)}, s32[]{:S(2)}) async-start(s8[9437184]{0:T(1024)(128)(4,1)} %bitcast.286), calls=%async_computation.30 | async-start | bytes 8388608
  67.1 17.8 %copy-start.6 = (f32[256,768]{1,0:T(8,128)}, f32[256,768]{1,0:T(8,128)S(1)}, u32[]{:S(2)}) copy-start(f32[256,768]{1,0:T(8,128)S(1)} %get-tuple-element.240) | copy-start | bytes 2359300
  67.1 17.7 %copy-start.75 = (f32[256]{0:T(256)}, f32[256]{0:T(256)S(1)}, u32[]{:S(2)}) copy-start(f32[256]{0:T(256)S(1)} %broadcast_multiply_fusion.8) | copy-start | bytes 3076
  67.4 17.5 %copy-start.88 = (f32[256]{0:T(256)}, f32[256]{0:T(256)S(1)}, u32[]{:S(2)}) copy-start(f32[256]{0:T(256)S(1)} %add_rsqrt_fusion) | copy-start | bytes 3076
  92.4 22.7 %reduce-scatter.19.cloned.1.call-start = ((), (), s32[]{:S(2)}) async-start(), calls=%async_computation.9 | async-start | bytes 1179648 | tf_op jit(solution)/shard_map/reduce_scatter | solution.py:250
  101.9 68.1 %reduce-scatter.25.cloned.1.call-start = ((), (), s32[]{:S(2)}) async-start(), calls=%async_computation.12 | async-start | bytes 1179648 | tf_op jit(solution)/shard_map/reduce_scatter | solution.py:253
  115.2 12.1 %slice-start.6 = ((s8[9437184]{0:T(1024)(128)(4,1)}), s8[4194304]{0:T(1024)(128)(4,1)S(1)}, s32[]{:S(2)}) async-start(s8[9437184]{0:T(1024)(128)(4,1)} %bitcast.282), calls=%async_computation.24 | async-start | bytes 8388608
  137.0 33.0 %reduce-scatter.23.cloned.1.call-start = ((), (), s32[]{:S(2)}) async-start(), calls=%async_computation.11 | async-start | bytes 1179648 | tf_op jit(solution)/shard_map/reduce_scatter | solution.py:250
  146.3 115.2 %reduce-scatter.35.cloned.1.call-start = ((), (), s32[]{:S(2)}) async-start(), calls=%async_computation.17 | async-start | bytes 1622016
  156.1 217.4 %reduce-scatter.29.cloned.1.call-start = ((), (), s32[]{:S(2)}) async-start(), calls=%async_computation.14 | async-start | bytes 4866048 | tf_op jit(solution)/shard_map/reduce_scatter | solution.py:290
  161.2 381.9 %reduce-scatter.27.cloned.1.call-start = ((), (), s32[]{:S(2)}) async-start(), calls=%async_computation.13 | async-start | bytes 14598144 | tf_op jit(solution)/shard_map/reduce_scatter | solution.py:288
  186.7 568.5 %reduce-scatter.31.cloned.1.call-start = ((), (), s32[]{:S(2)}) async-start(), calls=%async_computation.15 | async-start | bytes 19464192 | tf_op jit(solution)/shard_map/reduce_scatter | solution.py:294
  199.5 767.9 %reduce-scatter.33.cloned.1.call-start = ((), (), s32[]{:S(2)}) async-start(), calls=%async_computation.16 | async-start | bytes 19464192 | tf_op jit(solution)/shard_map/reduce_scatter | solution.py:296
  215.5 48.7 %copy-start.41 = (bf16[256,12,64]{0,2,1:T(8,128)(2,1)S(1)}, bf16[256,12,64]{0,2,1:T(8,128)(2,1)}, u32[]{:S(2)}) copy-start(bf16[256,12,64]{0,2,1:T(8,128)(2,1)} %get-tuple-element.224) | copy-start | bytes 1179652
  215.5 48.7 %copy-start.68 = (f32[256]{0:T(256)S(1)}, f32[256]{0:T(256)}, u32[]{:S(2)}) copy-start(f32[256]{0:T(256)} %copy-done.66) | copy-start | bytes 3076
  264.2 49.2 %copy-start.3 = (f32[256,768]{1,0:T(8,128)S(1)}, f32[256,768]{1,0:T(8,128)}, u32[]{:S(2)}) copy-start(f32[256,768]{1,0:T(8,128)} %copy-done.2) | copy-start | bytes 2359300
  264.2 49.2 %copy-start.81 = (f32[256]{0:T(256)S(1)}, f32[256]{0:T(256)}, u32[]{:S(2)}) copy-start(f32[256]{0:T(256)} %copy-done.79) | copy-start | bytes 3076
  (92 other events, 346.0 us)
Sparse Core Ops, SparseCore 0:
  92.5 10.8 reduce-scatter.20
  105.7 9.3 reduce-scatter.18
  137.1 9.4 reduce-scatter.24
  148.7 9.4 reduce-scatter.22
  163.3 98.1 reduce-scatter.34
  267.4 106.0 reduce-scatter.28
  381.1 161.8 reduce-scatter.26
  551.2 203.9 reduce-scatter.30
  763.3 203.9 reduce-scatter.32
where the time goes:
time: 978 us; the launch traced here: 974 us
  waiting for transfers between devices  695 us (71%)
  matrix products  115 us (12%)
  other arithmetic  55.6 us (6%)
  blocking collectives  53.1 us (5%)
  local copies, waits for them, and re-layouts  38.6 us (4%)
  between operations  15.4 us (2%)
    reduce_scatter x1, waiting for transfers between devices, body(): lax.psum_scatter(stacked[10], ('row', 'tok'), scatter_dimension=1, tiled=...  212 us
    reduce_scatter x1, waiting for transfers between devices, body(): lax.psum_scatter(stacked[8], ('row', 'tok'), scatter_dimension=1, tiled=T...  212 us
    reduce_scatter x1, waiting for transfers between devices, body(): lax.psum_scatter(stacked[2], ('row', 'tok'), scatter_dimension=1, tiled=T...  170 us
    reduce_scatter x1, waiting for transfers between devices, body(): lax.psum_scatter(stacked[4], ('row', 'tok'), scatter_dimension=1, tiled=T...  58.9 us
    unnamed x1, blocking collectives  41 us
    another operation x14, other arithmetic, body(): jnp.stack([gradients[layer_index][position] for layer_index in range(laye...  34 us
    unnamed x10, waiting for transfers between devices  33.7 us
    dot_general x8, matrix products, left_product(): jnp.einsum('ti,tj->ij', left, right, preferred_element_type=jnp.float32)  26 us
  transfers between devices with their start and end apart: 9, of which 6 were waited for; matrix products, arithmetic and copies ran while one was open for 11% of the time, Pallas kernels for 0%

commit v1 on v0

v1 whole, which is shorter than its diff:
```python
import jax
import jax.numpy as jnp
from jax import lax
from jax.sharding import PartitionSpec as P

epsilon = 1e-05
score_scale = 0.125
masked_score = -1e30


def normalize(stream):
    centre = stream - jnp.mean(stream, axis=-1, keepdims=True)
    inverse = lax.rsqrt(jnp.mean(centre * centre, axis=-1, keepdims=True) + epsilon)
    return (centre * inverse, inverse)


def norm_back(upstream, unit, inverse, gain):
    scaled = upstream * gain
    return inverse * (
        scaled
        - jnp.mean(scaled, axis=-1, keepdims=True)
        - unit * jnp.mean(scaled * unit, axis=-1, keepdims=True)
    )


def gelu_exact(preact):
    return jax.nn.gelu(preact, approximate=False)


def left_product(left, right):
    return jnp.einsum("ti,tj->ij", left, right, preferred_element_type=jnp.float32)


def right_product(left, right):
    return jnp.einsum("tj,ij->ti", left, right, preferred_element_type=jnp.float32)


def swap_cores(array):
    return lax.ppermute(array, "tok", [(0, 1), (1, 0)])


def pair_rows(array, core):
    other = swap_cores(array)
    first = jnp.where(core == 0, array, other)
    second = jnp.where(core == 0, other, array)
    return jnp.concatenate([first, second], axis=0)


def halve(parts, bit, chips, me):
    array, bits = parts
    axis = bits.index(bit)
    mine = (me >> bit) & 1
    sent = lax.dynamic_index_in_dim(array, 1 - mine, axis, keepdims=False)
    kept = lax.dynamic_index_in_dim(array, mine, axis, keepdims=False)
    pairs = [(chip, chip ^ (1 << bit)) for chip in range(chips)]
    received = lax.ppermute(sent, "row", pairs)
    summed = kept.astype(jnp.float32) + received.astype(jnp.float32)
    return (summed, bits[:axis] + bits[axis + 1 :])


def chip_sum(array, order, chips, me):
    bits = tuple(reversed(range(chips.bit_length() - 1)))
    kind = array.dtype
    parts = (array.reshape((2,) * len(bits) + array.shape[1:]), bits)
    for bit in order:
        parts = halve((parts[0].astype(kind), parts[1]), bit, chips, me)
    return parts[0]


def body(
    tokens,
    cotangent,
    segment_ids,
    valid,
    first_gain,
    first_shift,
    joint_weight,
    joint_bias,
    output_weight,
    output_bias,
    second_gain,
    second_shift,
    up_weight,
    up_bias,
    down_weight,
    down_bias,
    chips,
):
    layers, width = joint_weight.shape[:2]
    heads = width // 64
    rows = tokens.shape[1]
    core = lax.axis_index("tok")
    me = lax.axis_index("row")
    count = chips.bit_length() - 1
    rest = tuple(range(2, count))
    by_x = (0, 1) + rest
    by_y = (1, 0) + rest
    by_z = (2, 0, 1) + tuple(range(3, count))

    code_local = segment_ids[0] * 2 + valid[0]
    code_all = pair_rows(code_local, core)
    allowed = (code_local[:, None] == code_all[None, :])[None]

    def split_heads(array):
        return array.reshape(array.shape[0], heads, -1)

    def weight_sum(left, right, order):
        half = right.shape[1] // 2
        sent = lax.dynamic_slice_in_dim(right, (1 - core) * half, half, axis=1)
        kept = lax.dynamic_slice_in_dim(right, core * half, half, axis=1)
        left_all = jnp.concatenate([left, swap_cores(left)], axis=0)
        right_all = jnp.concatenate([kept, swap_cores(sent)], axis=0)
        product = left_product(left_all, right_all).astype(jnp.bfloat16)
        product = product.reshape(chips, -1, half)
        total = chip_sum(product, order, chips, me)
        total = total.reshape(2, -1, half)
        sent = lax.dynamic_index_in_dim(total, 1 - core, 0, keepdims=False)
        kept = lax.dynamic_index_in_dim(total, core, 0, keepdims=False)
        other = swap_cores(sent)
        return jnp.where(
            core == 0,
            jnp.concatenate([kept, other], axis=1),
            jnp.concatenate([other, kept], axis=1),
        )

    stream = tokens[0].astype(jnp.float32)
    saved = []
    for layer in range(layers):
        unit_one, inverse_one = normalize(stream)
        normed_one = (unit_one * first_gain[layer] + first_shift[layer]).astype(jnp.bfloat16)
        mixed = jnp.dot(normed_one, joint_weight[layer], preferred_element_type=jnp.float32)
        queries = (mixed[:, :width] + joint_bias[layer, 0]).astype(jnp.bfloat16)
        key_rows = mixed[:, width : 2 * width].astype(jnp.bfloat16)
        value_rows = (mixed[:, 2 * width :] + joint_bias[layer, 1]).astype(jnp.bfloat16)
        both = pair_rows(jnp.concatenate([key_rows, value_rows], axis=1), core)
        queries = split_heads(queries)
        key_all = split_heads(both[:, :width])
        value_all = split_heads(both[:, width:])
        scores = (
            jnp.einsum("qhd,khd->hqk", queries, key_all, preferred_element_type=jnp.float32)
            * score_scale
        )
        scores = jnp.where(allowed, scores, masked_score)
        exponent = jnp.exp(scores - jnp.max(scores, axis=-1, keepdims=True))
        soft = exponent / jnp.sum(exponent, axis=-1, keepdims=True)
        soft_low = soft.astype(jnp.bfloat16)
        attended = jnp.einsum(
            "hqk,khd->qhd", soft_low, value_all, preferred_element_type=jnp.float32
        )
        attended = attended.reshape(rows, width).astype(jnp.bfloat16)
        middle = (
            stream
            + jnp.dot(attended, output_weight[layer], preferred_element_type=jnp.float32)
            + output_bias[layer]
        )
        unit_two, inverse_two = normalize(middle)
        normed_two = (unit_two * second_gain[layer] + second_shift[layer]).astype(jnp.bfloat16)
        preact = (
            jnp.dot(normed_two, up_weight[layer], preferred_element_type=jnp.float32)
            + up_bias[layer]
        )
        hidden = gelu_exact(preact).astype(jnp.bfloat16)
        stream = (
            middle
            + jnp.dot(hidden, down_weight[layer], preferred_element_type=jnp.float32)
            + down_bias[layer]
        )
        saved.append(
            (unit_one, inverse_one, normed_one, queries, key_all, value_all, soft, attended)
            + (unit_two, inverse_two, normed_two, preact, hidden)
        )
    output = stream.astype(jnp.bfloat16)[None]
    upstream = cotangent[0].astype(jnp.float32)
    small = [None] * layers
    large = [None] * layers
    for layer in reversed(range(layers)):
        (unit_one, inverse_one, normed_one, queries, key_all, value_all, soft, attended) = saved[
            layer
        ][:8]
        unit_two, inverse_two, normed_two, preact, hidden = saved[layer][8:]
        turn = (layers - 1 - layer) % 2
        up_low = upstream.astype(jnp.bfloat16)
        down_bias_grad = jnp.sum(upstream, axis=0)
        down_weight_grad = weight_sum(hidden, up_low, by_y if turn else by_x)
        hidden_grad = right_product(up_low, down_weight[layer])
        preact_grad = jax.vjp(gelu_exact, preact)[1](hidden_grad)[0]
        up_bias_grad = jnp.sum(preact_grad, axis=0)
        preact_low = preact_grad.astype(jnp.bfloat16)
        up_weight_grad = weight_sum(normed_two, preact_low, by_x if turn else by_y)
        normed_two_grad = right_product(preact_low, up_weight[layer])
        second_gain_grad = jnp.sum(normed_two_grad * unit_two, axis=0)
        second_shift_grad = jnp.sum(normed_two_grad, axis=0)
        middle_grad = upstream + norm_back(
            normed_two_grad, unit_two, inverse_two, second_gain[layer]
        )
        middle_low = middle_grad.astype(jnp.bfloat16)
        output_bias_grad = jnp.sum(middle_grad, axis=0)
        output_weight_grad = weight_sum(attended, middle_low, by_z)
        attended_grad = split_heads(
            right_product(middle_low, output_weight[layer]).astype(jnp.bfloat16)
        )
        soft_low = soft.astype(jnp.bfloat16)
        soft_grad = jnp.einsum(
            "qhd,khd->hqk", attended_grad, value_all, preferred_element_type=jnp.float32
        )
        delta = jnp.sum(soft_grad * soft, axis=-1, keepdims=True)
        score_grad = (soft * (soft_grad - delta)).astype(jnp.bfloat16)
        query_grad = (
            jnp.einsum("hqk,khd->qhd", score_grad, key_all, preferred_element_type=jnp.float32)
            * score_scale
        ).reshape(rows, width)
        key_grad = (
            jnp.einsum("hqk,qhd->khd", score_grad, queries, preferred_element_type=jnp.float32)
            * score_scale
        )
        value_grad = jnp.einsum(
            "hqk,qhd->khd", soft_low, attended_grad, preferred_element_type=jnp.float32
        )
        both = jnp.concatenate(
            [key_grad.reshape(2 * rows, width), value_grad.reshape(2 * rows, width)], axis=1
        )
        both = both.reshape(2, rows, 2 * width)
        sent = lax.dynamic_index_in_dim(both, 1 - core, 0, keepdims=False)
        kept = lax.dynamic_index_in_dim(both, core, 0, keepdims=False)
        both = kept + swap_cores(sent.astype(jnp.bfloat16)).astype(jnp.float32)
        joint_bias_grad = jnp.stack(
            [jnp.sum(query_grad, axis=0), jnp.sum(both[:, width:], axis=0)]
        )
        mixed_low = jnp.concatenate([query_grad, both], axis=1).astype(jnp.bfloat16)
        joint_weight_grad = weight_sum(normed_one, mixed_low, by_z)
        normed_one_grad = right_product(mixed_low, joint_weight[layer])
        first_gain_grad = jnp.sum(normed_one_grad * unit_one, axis=0)
        first_shift_grad = jnp.sum(normed_one_grad, axis=0)
        upstream = middle_grad + norm_back(
            normed_one_grad, unit_one, inverse_one, first_gain[layer]
        )
        small[layer] = (
            first_gain_grad,
            first_shift_grad,
            joint_bias_grad[0],
            joint_bias_grad[1],
            output_bias_grad,
            second_gain_grad,
            second_shift_grad,
            down_bias_grad,
            up_bias_grad,
        )
        large[layer] = (joint_weight_grad, output_weight_grad, up_weight_grad, down_weight_grad)

    pieces = [vector.reshape(chips, 2, -1) for layer in range(layers) for vector in small[layer]]
    packed = jnp.concatenate(pieces, axis=2)
    sent = lax.dynamic_index_in_dim(packed, 1 - core, 1, keepdims=False)
    kept = lax.dynamic_index_in_dim(packed, core, 1, keepdims=False)
    packed = chip_sum(kept + swap_cores(sent), by_x, chips, me)
    vectors, at = [], 0
    for piece in pieces:
        vectors.append(packed[at : at + piece.shape[2]])
        at += piece.shape[2]
    per = len(small[0])

    def stacked(position):
        return jnp.stack([vectors[layer * per + position] for layer in range(layers)])

    def matrix(position):
        return jnp.stack([large[layer][position] for layer in range(layers)])

    return (
        output,
        upstream[None],
        stacked(0),
        stacked(1),
        matrix(0),
        jnp.stack([stacked(2), stacked(3)], axis=1),
        matrix(1),
        stacked(4),
        stacked(5),
        stacked(6),
        matrix(2),
        stacked(8),
        matrix(3),
        stacked(7),
    )


def solution(mesh):
    chips = mesh.shape["row"]
    split = P("row", "tok", None)
    in_specs = (split, split, P("row", "tok"), P("row", "tok")) + (P(),) * 12
    vector = P(None, ("row", "tok"))
    table = P(None, ("row", "tok"), None)
    out_specs = (
        split,
        split,
        vector,
        vector,
        table,
        P(None, None, ("row", "tok")),
        table,
        vector,
        vector,
        vector,
        table,
        vector,
        table,
        vector,
    )

    def run(*arrays):
        return body(*arrays, chips=chips)

    return jax.shard_map(run, mesh=mesh, in_specs=in_specs, out_specs=out_specs, check_vma=False)
```

time: 978 us -> 479 us (0.49)
  waiting for transfers between devices: 695 us -> 146 us
  starting transfers between devices: 1.16 us -> 62.3 us
  blocking collectives: 53.1 us -> 0 us
  local copies, waits for them, and re-layouts: 38.6 us -> 85.4 us
  between operations: 15.4 us -> 3.31 us
  matrix products: 115 us -> 127 us
    reduce_scatter x8 -> x0, waiting for transfers between devices: 662 us -> none  [the longest x1 212 us: body(): lax.psum_scatter(stacked[10], ('row', 'tok'), scatter_dimension=1, tiled=...]
    ppermute x0 -> x66, waiting for transfers between devices: none -> 146 us  [the longest x36 144 us: halve(): received = lax.ppermute(sent, 'row', pairs)]
    ppermute x0 -> x66, starting transfers between devices: none -> 62.3 us  [the longest x36 55.7 us: halve(): received = lax.ppermute(sent, 'row', pairs)]
    unnamed x1 -> x0, blocking collectives: 41 us -> none
    unnamed x10 -> x0, waiting for transfers between devices: 33.7 us -> none
    concatenate x0 -> x9, local copies, waits for them, and re-layouts: none -> 28.8 us  [the longest x8 27.6 us: body(): jnp.concatenate([key_grad.reshape(2 * rows, width), value_grad.reshape(2...]
    another operation x14 -> x16, other arithmetic: 34 us -> 11.2 us  [the longest x7 3.99 us: stacked(): jnp.stack([vectors[layer * per + position] for layer in range(layers)])]
    reshape x0 -> x17, local copies, waits for them, and re-layouts: none -> 21.9 us  [the longest x14 17.3 us: body(): vector.reshape(chips, 2, -1)]
  transfers between devices with their start and end apart: 9 -> 66, of which waited for: 6 -> 21; matrix products, arithmetic and copies ran while one was open for 11% -> 46% of each run, Pallas kernels for 0% -> 0%
where the time goes in v1:
time: 479 us; the launch traced here: 472 us
  waiting for transfers between devices  146 us (30%)
  matrix products  127 us (27%)
  local copies, waits for them, and re-layouts  85.4 us (18%)
  starting transfers between devices  62.3 us (13%)
  other arithmetic  47.6 us (10%)
    ppermute x36, waiting for transfers between devices, halve(): received = lax.ppermute(sent, 'row', pairs)  144 us
    ppermute x36, starting transfers between devices, halve(): received = lax.ppermute(sent, 'row', pairs)  55.7 us
    concatenate x8, local copies, waits for them, and re-layouts, body(): jnp.concatenate([key_grad.reshape(2 * rows, width), value_grad.reshape(2...  27.6 us
    dot_general x8, matrix products, left_product(): jnp.einsum('ti,tj->ij', left, right, preferred_element_type=jnp.float32)  23.5 us
    dot_general x8, matrix products, right_product(): jnp.einsum('tj,ij->ti', left, right, preferred_element_type=jnp.float32)  22.4 us
    dot_general x2, matrix products, body(): jnp.dot(normed_two, up_weight[layer], preferred_element_type=jnp.float32)  19.8 us
    reshape x14, local copies, waits for them, and re-layouts, body(): vector.reshape(chips, 2, -1)  17.3 us
    sub x2, matrix products, body(): exponent = jnp.exp(scores - jnp.max(scores, axis=-1, keepdims=True))  11.6 us
  transfers between devices with their start and end apart: 66, of which 21 were waited for; matrix products, arithmetic and copies ran while one was open for 46% of the time, Pallas kernels for 0%

profile of v1, /device:TPU:0, one launch (start us, length us, event | category | flops | bytes accessed | tf_op | source)
XLA Modules:
  0.0 471.7 jit_solution(1708377573929439680)
XLA Ops:
  5.9 3.3 fusion.40
  13.1 4.8 %fusion.273 = (f32[12,256]{1,0:T(8,128)S(1)}, f32[12,256,512]{2,1,0:T(8,128)}) fusion(pred[256,512]{1,0:T(8,128)(4,1)S(1)} %broadcast_compare_fusion, bf16[256,12,64]{0,2,1:T(8,128)(2,1)S(1)} %bitcast.506, bf16[512,12,64]{0,2,1:T(8,128)(2,1)S(1)} %bitcast.490), kind=kOutput, calls=%fused_computation.537 | convolution fusion | flops 207618560 | bytes 7614464 | tf_op jit(solution)/shard_map/sub | solution.py:144
  18.0 4.8 %fusion.129 = bf16[12,64,256]{2,1,0:T(8,128)(2,1)} fusion(bf16[512,12,64]{0,2,1:T(8,128)(2,1)S(1)} %bitcast.518, f32[12,256,512]{2,1,0:T(8,128)} %get-tuple-element.175, f32[12,256]{1,0:T(8,128)S(1)} %get-tuple-element.174), kind=kOutput, calls=%fused_computation.181 | convolution fusion | flops 204668928 | bytes 7483392 | tf_op jit(solution)/shard_map/hqk,khd->qhd/dot_general | solution.py:147
  25.7 10.1 %multiply_convert_fusion.3 = (bf16[256,3072]{1,0:T(8,128)(2,1)}, f32[256,3072]{1,0:T(8,128)}, f32[256,3072]{1,0:T(8,128)}) fusion(f32[3072]{0:T(1024)S(1)} %bitcast.541, bf16[256,768]{1,0:T(8,128)(2,1)S(1)} %add_convert_fusion.2, bf16[2,768,3072]{2,1,0:T(8,128)(2,1)S(1)} %bitcast.554), kind=kOutput, calls=%fused_computation.86 | convolution fusion | flops 1259864064 | bytes 12988416 | tf_op jit(solution)/shard_map/dot_general | solution.py:159
  48.9 6.7 %fusion.276 = (f32[12,256]{1,0:T(8,128)}, f32[12,256,512]{2,1,0:T(8,128)}) fusion(pred[256,512]{1,0:T(8,128)(4,1)} %copy-done.66, bf16[256,12,64]{0,2,1:T(8,128)(2,1)S(1)} %bitcast.508, bf16[512,12,64]{0,2,1:T(8,128)(2,1)S(1)} %bitcast.492), kind=kOutput, calls=%fused_computation.540 | convolution fusion | flops 207618560 | bytes 7614464 | tf_op jit(solution)/shard_map/sub | solution.py:144
  55.7 4.9 %fusion.132 = bf16[12,64,256]{2,1,0:T(8,128)(2,1)} fusion(bf16[512,12,64]{0,2,1:T(8,128)(2,1)S(1)} %bitcast.520, f32[12,256,512]{2,1,0:T(8,128)} %get-tuple-element.182, f32[12,256]{1,0:T(8,128)} %get-tuple-element.181), kind=kOutput, calls=%fused_computation.182 | convolution fusion | flops 204668928 | bytes 7483392 | tf_op jit(solution)/shard_map/hqk,khd->qhd/dot_general | solution.py:147
  63.3 9.7 %multiply_convert_fusion.2 = (bf16[256,3072]{1,0:T(8,128)(2,1)}, f32[256,3072]{1,0:T(8,128)S(1)}, f32[256,3072]{1,0:T(8,128)}) fusion(f32[3072]{0:T(1024)S(1)} %bitcast.540, bf16[256,768]{1,0:T(8,128)(2,1)S(1)} %add_convert_fusion, bf16[2,768,3072]{2,1,0:T(8,128)(2,1)S(1)} %bitcast.556), kind=kOutput, calls=%fused_computation.72 | convolution fusion | flops 1259864064 | bytes 12988416 | tf_op jit(solution)/shard_map/dot_general | solution.py:159
  73.0 4.6 fusion.268
  82.4 3.7 multiply_reduce_fusion.1
  86.2 5.5 %fusion.107 = f32[512,12,64]{0,2,1:T(8,128)} fusion(bf16[256,12,64]{0,2,1:T(8,128)(2,1)S(1)} %bitcast.527, f32[12,256,512]{2,1,0:T(8,128)} %get-tuple-element.182, f32[12,256]{1,0:T(8,128)S(1)} %copy-done.90), kind=kOutput, calls=%fused_computation.161 | convolution fusion | flops 204472320 | bytes 8269824 | tf_op jit(solution)/shard_map/hqk,qhd->khd/dot_general | solution.py:216
  93.0 3.6 fusion.135
  102.7 3.7 copy.55
  109.4 3.9 copy.54
  140.8 4.2 multiply_reduce_fusion.3
  146.9 5.5 %fusion.269 = (f32[3072]{0:T(1024)}, bf16[256,3072]{1,0:T(8,128)(2,1)S(1)}) fusion(f32[256,3072]{1,0:T(8,128)S(1)} %copy-done.114, f32[256,3072]{1,0:T(8,128)S(1)} %copy-done.115, bf16[256,768]{1,0:T(8,128)(2,1)S(1)} %convert_element_type.542, bf16[2,3072,768]{2,1,0:T(8,128)(2,1)} %param.30), kind=kOutput, calls=%fused_computation.533 | convolution fusion | flops 1219752960 | bytes 12988416 | tf_op jit(solution)/shard_map/tj,ij->ti/dot_general | solution.py:35
  159.0 4.0 multiply_reduce_fusion
  165.1 3.4 multiply_convert_fusion
  173.0 3.0 concatenate.276
  176.1 3.7 copy.59
  182.8 4.1 copy.58
  230.1 3.8 convolution_convert_fusion.1
  258.7 5.6 %convolution_convert_fusion = bf16[3072,384]{1,0:T(8,128)(2,1)} fusion(bf16[256,3072]{1,0:T(8,128)(2,1)} %collective-permute-done.59, bf16[256,3072]{1,0:T(8,128)(2,1)} %get-tuple-element.86, bf16[256,384]{1,0:T(8,128)(2,1)} %collective-permute-done.60, bf16[256,384]{1,0:T(8,128)(2,1)} %get-tuple-element.121), kind=kOutput, calls=%fused_computation.30 | convolution fusion | flops 1216217088 | bytes 5898240 | tf_op jit(solution)/shard_map/ti,tj->ij/dot_general | solution.py:31
  266.1 4.1 convolution_convert_fusion.3
  280.4 16.7 %collective-permute-done.7 = f32[2,2,576]{2,1,0:T(2,128)S(1)} collective-permute-done((f32[2,2,576]{2,1,0:T(2,128)S(1)}, f32[2,2,576]{2,1,0:T(2,128)S(1)}, u32[]{:S(2)}, u32[]{:S(2)}) %collective-permute-start.7) | collective-permute-done | bytes 9248 | tf_op jit(solution)/shard_map/ppermute | solution.py:56
  322.5 54.5 %collective-permute-done.48 = bf16[2,2,48,1536]{3,2,1,0:T(8,128)(2,1)S(1)} collective-permute-done((bf16[2,2,48,1536]{3,2,1,0:T(8,128)(2,1)S(1)}, bf16[2,2,48,1536]{3,2,1,0:T(8,128)(2,1)S(1)}, u32[]{:S(2)}, u32[]{:S(2)}) %collective-permute-start.48) | collective-permute-done | bytes 589856 | tf_op jit(solution)/shard_map/ppermute | solution.py:56
  378.2 20.5 %collective-permute-done.20 = bf16[2,2,48,1152]{3,2,1,0:T(8,128)(2,1)S(1)} collective-permute-done((bf16[2,2,48,1152]{3,2,1,0:T(8,128)(2,1)S(1)}, bf16[2,2,48,1152]{3,2,1,0:T(8,128)(2,1)S(1)}, u32[]{:S(2)}, u32[]{:S(2)}) %collective-permute-start.20) | collective-permute-done | bytes 442400 | tf_op jit(solution)/shard_map/ppermute | solution.py:56
  412.0 5.6 %collective-permute-done.50 = bf16[48,1536]{1,0:T(8,128)(2,1)S(1)} collective-permute-done((bf16[48,1536]{1,0:T(8,128)(2,1)S(1)}, bf16[48,1536]{1,0:T(8,128)(2,1)S(1)}, u32[]{:S(2)}, u32[]{:S(2)}) %collective-permute-start.50) | collective-permute-done | bytes 147488 | tf_op jit(solution)/shard_map/ppermute | solution.py:56
  417.6 3.4 collective-permute-start.22
  428.9 6.9 %collective-permute-done.57 = bf16[192,384]{1,0:T(8,128)(2,1)S(1)} collective-permute-done((bf16[192,384]{1,0:T(8,128)(2,1)S(1)}, bf16[192,384]{1,0:T(8,128)(2,1)S(1)}, u32[]{:S(2)}, u32[]{:S(2)}) %collective-permute-start.57) | collective-permute-done | bytes 147488 | tf_op jit(solution)/shard_map/ppermute | solution.py:56
  439.7 6.3 %collective-permute-done.42 = bf16[2,48,1536]{2,1,0:T(8,128)(2,1)S(1)} collective-permute-done((bf16[2,48,1536]{2,1,0:T(8,128)(2,1)S(1)}, bf16[2,48,1536]{2,1,0:T(8,128)(2,1)S(1)}, u32[]{:S(2)}, u32[]{:S(2)}) %collective-permute-start.42) | collective-permute-done | bytes 294944 | tf_op jit(solution)/shard_map/ppermute | solution.py:56
  447.3 7.8 %collective-permute-done.63 = bf16[2,192,384]{2,1,0:T(8,128)(2,1)S(1)} collective-permute-done((bf16[2,192,384]{2,1,0:T(8,128)(2,1)S(1)}, bf16[2,192,384]{2,1,0:T(8,128)(2,1)S(1)}, u32[]{:S(2)}, u32[]{:S(2)}) %collective-permute-start.63) | collective-permute-done | bytes 294944 | tf_op jit(solution)/shard_map/ppermute | solution.py:56
  458.5 8.0 %collective-permute-done.64 = bf16[192,384]{1,0:T(8,128)(2,1)S(1)} collective-permute-done((bf16[192,384]{1,0:T(8,128)(2,1)S(1)}, bf16[192,384]{1,0:T(8,128)(2,1)S(1)}, u32[]{:S(2)}, u32[]{:S(2)}) %collective-permute-start.64) | collective-permute-done | bytes 147488 | tf_op jit(solution)/shard_map/ppermute | solution.py:56
  (646 shorter events, 227.8 us)
Async XLA Ops:
  44.5 211.7 %collective-permute-start.60 = (bf16[256,384]{1,0:T(8,128)(2,1)}, bf16[256,384]{1,0:T(8,128)(2,1)}, u32[]{:S(2)}, u32[]{:S(2)}) collective-permute-start(bf16[256,384]{1,0:T(8,128)(2,1)} %get-tuple-element.122), channel_id=1, source_target_pairs={{0,1},{1,0},{2,3},{3,2},{4,5},{5,4},{6,7},{7,6},{8,9},{9,8},{10,11... | collective-permute-start | bytes 589832 | tf_op jit(solution)/shard_map/ppermute | solution.py:39
  44.6 190.7 %collective-permute-start.17 = (bf16[256,768]{1,0:T(8,128)(2,1)}, bf16[256,768]{1,0:T(8,128)(2,1)}, u32[]{:S(2)}, u32[]{:S(2)}) collective-permute-start(bf16[256,768]{1,0:T(8,128)(2,1)} %add_convert_fusion.1), channel_id=1, source_target_pairs={{0,1},{1,0},{2,3},{3,2},{4,5},{5,4},{6,7},{7,6},{8,9},{9,8},{10,11... | collective-permute-start | bytes 1179656 | tf_op jit(solution)/shard_map/ppermute | solution.py:39
  45.0 161.4 %collective-permute-start.24 = (bf16[256,768]{0,1:T(8,128)(2,1)}, bf16[256,768]{0,1:T(8,128)(2,1)}, u32[]{:S(2)}, u32[]{:S(2)}) collective-permute-start(bf16[256,768]{0,1:T(8,128)(2,1)} %bitcast.8), channel_id=1, source_target_pairs={{0,1},{1,0},{2,3},{3,2},{4,5},{5,4},{6,7},{7,6},{8,9},{9,8},{10,11... | collective-permute-start | bytes 1179656 | tf_op jit(solution)/shard_map/ppermute | solution.py:39
  91.7 24.4 %collective-permute-start.31 = (bf16[256,768]{0,1:T(8,128)(2,1)}, bf16[256,768]{0,1:T(8,128)(2,1)}, u32[]{:S(2)}, u32[]{:S(2)}) collective-permute-start(bf16[256,768]{0,1:T(8,128)(2,1)} %bitcast.18), channel_id=1, source_target_pairs={{0,1},{1,0},{2,3},{3,2},{4,5},{5,4},{6,7},{7,6},{8,9},{9,8},{10,11... | collective-permute-start | bytes 1179656 | tf_op jit(solution)/shard_map/ppermute | solution.py:39
  92.9 22.9 %collective-permute-start.32 = (bf16[256,384]{1,0:T(8,128)(2,1)}, bf16[256,384]{1,0:T(8,128)(2,1)}, u32[]{:S(2)}, u32[]{:S(2)}) collective-permute-start(bf16[256,384]{1,0:T(8,128)(2,1)} %get-tuple-element.126), channel_id=1, source_target_pairs={{0,1},{1,0},{2,3},{3,2},{4,5},{5,4},{6,7},{7,6},{8,9},{9,8},{10,11... | collective-permute-start | bytes 589832 | tf_op jit(solution)/shard_map/ppermute | solution.py:39
  115.8 21.8 %collective-permute-start.3 = (bf16[256,1536]{1,0:T(8,128)(2,1)}, bf16[256,1536]{1,0:T(8,128)(2,1)}, u32[]{:S(2)}, u32[]{:S(2)}) collective-permute-start(bf16[256,1536]{1,0:T(8,128)(2,1)} %fusion.180), channel_id=1, source_target_pairs={{0,1},{1,0},{2,3},{3,2},{4,5},{5,4},{6,7},{7,6},{8,9},{9,8},{10,11... | collective-permute-start | bytes 2359304 | tf_op jit(solution)/shard_map/ppermute | solution.py:39
  119.4 16.3 %collective-permute-start.33 = (bf16[2,2,2,48,384]{4,3,2,1,0:T(8,128)(2,1)}, bf16[2,2,2,48,384]{4,3,2,1,0:T(8,128)(2,1)}, u32[]{:S(2)}, u32[]{:S(2)}) collective-permute-start(bf16[2,2,2,48,384]{4,3,2,1,0:T(8,128)(2,1)} %dynamic-slice_bitcast_fusion.16), channel_id=1, source_target_pairs={{0,8},{2,10},{4,12},{6,14},{8,0},{10,2},{12,4},{14,6},{16,24},{18,... | collective-permute-start | bytes 884744 | tf_op jit(solution)/shard_map/ppermute | solution.py:56
  135.7 54.2 %collective-permute-start.45 = (bf16[256,768]{1,0:T(8,128)(2,1)}, bf16[256,768]{1,0:T(8,128)(2,1)}, u32[]{:S(2)}, u32[]{:S(2)}) collective-permute-start(bf16[256,768]{1,0:T(8,128)(2,1)} %copy-done.60), channel_id=1, source_target_pairs={{0,1},{1,0},{2,3},{3,2},{4,5},{5,4},{6,7},{7,6},{8,9},{9,8},{10,11... | collective-permute-start | bytes 1179656 | tf_op jit(solution)/shard_map/ppermute | solution.py:39
  137.7 52.5 %collective-permute-start.46 = (bf16[256,1536]{1,0:T(8,128)(2,1)}, bf16[256,1536]{1,0:T(8,128)(2,1)}, u32[]{:S(2)}, u32[]{:S(2)}) collective-permute-start(bf16[256,1536]{1,0:T(8,128)(2,1)} %get-tuple-element.101), channel_id=1, source_target_pairs={{0,1},{1,0},{2,3},{3,2},{4,5},{5,4},{6,7},{7,6},{8,9},{9,8},{10,11... | collective-permute-start | bytes 2359304 | tf_op jit(solution)/shard_map/ppermute | solution.py:39
  190.0 38.5 %collective-permute-start.52 = (bf16[256,3072]{1,0:T(8,128)(2,1)}, bf16[256,3072]{1,0:T(8,128)(2,1)}, u32[]{:S(2)}, u32[]{:S(2)}) collective-permute-start(bf16[256,3072]{1,0:T(8,128)(2,1)} %get-tuple-element.88), channel_id=1, source_target_pairs={{0,1},{1,0},{2,3},{3,2},{4,5},{5,4},{6,7},{7,6},{8,9},{9,8},{10,11... | collective-permute-start | bytes 4718600 | tf_op jit(solution)/shard_map/ppermute | solution.py:39
  210.4 16.9 %collective-permute-start.26 = (bf16[2,2,2,48,384]{4,3,2,1,0:T(8,128)(2,1)}, bf16[2,2,2,48,384]{4,3,2,1,0:T(8,128)(2,1)}, u32[]{:S(2)}, u32[]{:S(2)}) collective-permute-start(bf16[2,2,2,48,384]{4,3,2,1,0:T(8,128)(2,1)} %dynamic-slice_bitcast_fusion.17), channel_id=1, source_target_pairs={{0,8},{2,10},{4,12},{6,14},{8,0},{10,2},{12,4},{14,6},{16,24},{18,... | collective-permute-start | bytes 884744 | tf_op jit(solution)/shard_map/ppermute | solution.py:56
  211.2 14.1 %collective-permute-start.37 = (f32[24,384]{1,0:T(8,128)}, f32[24,384]{1,0:T(8,128)}, u32[]{:S(2)}, u32[]{:S(2)}) collective-permute-start(f32[24,384]{1,0:T(8,128)} %get-tuple-element.145), channel_id=1, source_target_pairs={{0,1},{1,0},{2,3},{3,2},{4,5},{5,4},{6,7},{7,6},{8,9},{9,8},{10,11... | collective-permute-start | bytes 110600 | tf_op jit(solution)/shard_map/ppermute | solution.py:39
  225.3 40.3 %collective-permute-start.38 = (bf16[256,768]{1,0:T(8,128)(2,1)}, bf16[256,768]{1,0:T(8,128)(2,1)}, u32[]{:S(2)}, u32[]{:S(2)}) collective-permute-start(bf16[256,768]{1,0:T(8,128)(2,1)} %copy-done.58), channel_id=1, source_target_pairs={{0,1},{1,0},{2,3},{3,2},{4,5},{5,4},{6,7},{7,6},{8,9},{9,8},{10,11... | collective-permute-start | bytes 1179656 | tf_op jit(solution)/shard_map/ppermute | solution.py:39
  235.2 21.8 %collective-permute-start.59 = (bf16[256,3072]{1,0:T(8,128)(2,1)}, bf16[256,3072]{1,0:T(8,128)(2,1)}, u32[]{:S(2)}, u32[]{:S(2)}) collective-permute-start(bf16[256,3072]{1,0:T(8,128)(2,1)} %get-tuple-element.86), channel_id=1, source_target_pairs={{0,1},{1,0},{2,3},{3,2},{4,5},{5,4},{6,7},{7,6},{8,9},{9,8},{10,11... | collective-permute-start | bytes 4718600 | tf_op jit(solution)/shard_map/ppermute | solution.py:39
  245.4 64.9 %collective-permute-start.47 = (bf16[2,2,2,48,1536]{4,3,2,1,0:T(8,128)(2,1)}, bf16[2,2,2,48,1536]{4,3,2,1,0:T(8,128)(2,1)}, u32[]{:S(2)}, u32[]{:S(2)}) collective-permute-start(bf16[2,2,2,48,1536]{4,3,2,1,0:T(8,128)(2,1)} %dynamic-slice_bitcast_fusion.2), channel_id=1, source_target_pairs={{0,4},{2,6},{4,0},{6,2},{8,12},{10,14},{12,8},{14,10},{16,20},{18,... | collective-permute-start | bytes 3538952 | tf_op jit(solution)/shard_map/ppermute | solution.py:56
  247.4 18.2 %collective-permute-start.39 = (bf16[256,1536]{1,0:T(8,128)(2,1)}, bf16[256,1536]{1,0:T(8,128)(2,1)}, u32[]{:S(2)}, u32[]{:S(2)}) collective-permute-start(bf16[256,1536]{1,0:T(8,128)(2,1)} %get-tuple-element.99), channel_id=1, source_target_pairs={{0,1},{1,0},{2,3},{3,2},{4,5},{5,4},{6,7},{7,6},{8,9},{9,8},{10,11... | collective-permute-start | bytes 2359304 | tf_op jit(solution)/shard_map/ppermute | solution.py:39
  256.2 60.1 %collective-permute-start.54 = (bf16[2,2,2,192,384]{4,3,2,1,0:T(8,128)(2,1)}, bf16[2,2,2,192,384]{4,3,2,1,0:T(8,128)(2,1)}, u32[]{:S(2)}, u32[]{:S(2)}) collective-permute-start(bf16[2,2,2,192,384]{4,3,2,1,0:T(8,128)(2,1)} %dynamic-slice_bitcast_fusion.1), channel_id=1, source_target_pairs={{0,4},{2,6},{4,0},{6,2},{8,12},{10,14},{12,8},{14,10},{16,20},{18,... | collective-permute-start | bytes 3538952 | tf_op jit(solution)/shard_map/ppermute | solution.py:56
  257.0 62.9 %collective-permute-start.19 = (bf16[2,2,2,48,1152]{4,3,2,1,0:T(8,128)(2,1)}, bf16[2,2,2,48,1152]{4,3,2,1,0:T(8,128)(2,1)}, u32[]{:S(2)}, u32[]{:S(2)}) collective-permute-start(bf16[2,2,2,48,1152]{4,3,2,1,0:T(8,128)(2,1)} %dynamic-slice_bitcast_fusion.4), channel_id=1, source_target_pairs={{0,8},{2,10},{4,12},{6,14},{8,0},{10,2},{12,4},{14,6},{16,24},{18,... | collective-permute-start | bytes 2654216 | tf_op jit(solution)/shard_map/ppermute | solution.py:56
  265.6 31.6 %collective-permute-start.30 = (f32[24,384]{1,0:T(8,128)}, f32[24,384]{1,0:T(8,128)}, u32[]{:S(2)}, u32[]{:S(2)}) collective-permute-start(f32[24,384]{1,0:T(8,128)} %get-tuple-element.143), channel_id=1, source_target_pairs={{0,1},{1,0},{2,3},{3,2},{4,5},{5,4},{6,7},{7,6},{8,9},{9,8},{10,11... | collective-permute-start | bytes 110600 | tf_op jit(solution)/shard_map/ppermute | solution.py:39
  277.4 19.7 %collective-permute-start.7 = (f32[2,2,576]{2,1,0:T(2,128)S(1)}, f32[2,2,576]{2,1,0:T(2,128)S(1)}, u32[]{:S(2)}, u32[]{:S(2)}) collective-permute-start(f32[2,2,576]{2,1,0:T(2,128)S(1)} %bitcast.542), channel_id=1, source_target_pairs={{0,4},{2,6},{4,0},{6,2},{8,12},{10,14},{12,8},{14,10},{16,20},{18,... | collective-permute-start | bytes 27656 | tf_op jit(solution)/shard_map/ppermute | solution.py:56
  297.2 16.9 %collective-permute-start.11 = (bf16[256,1152]{1,0:T(8,128)(2,1)S(1)}, bf16[256,1152]{1,0:T(8,128)(2,1)S(1)}, u32[]{:S(2)}, u32[]{:S(2)}) collective-permute-start(bf16[256,1152]{1,0:T(8,128)(2,1)S(1)} %copy-done.56), channel_id=1, source_target_pairs={{0,1},{1,0},{2,3},{3,2},{4,5},{5,4},{6,7},{7,6},{8,9},{9,8},{10,11... | collective-permute-start | bytes 1769480 | tf_op jit(solution)/shard_map/ppermute | solution.py:39
  310.3 90.4 %collective-permute-start.40 = (bf16[2,2,2,48,1536]{4,3,2,1,0:T(8,128)(2,1)S(1)}, bf16[2,2,2,48,1536]{4,3,2,1,0:T(8,128)(2,1)S(1)}, u32[]{:S(2)}, u32[]{:S(2)}) collective-permute-start(bf16[2,2,2,48,1536]{4,3,2,1,0:T(8,128)(2,1)S(1)} %dynamic-slice_bitcast_fusion.3), channel_id=1, source_target_pairs={{0,2},{2,0},{4,6},{6,4},{8,10},{10,8},{12,14},{14,12},{16,18},{18,... | collective-permute-start | bytes 3538952 | tf_op jit(solution)/shard_map/ppermute | solution.py:56
  312.9 89.2 %collective-permute-start.61 = (bf16[2,2,2,192,384]{4,3,2,1,0:T(8,128)(2,1)S(1)}, bf16[2,2,2,192,384]{4,3,2,1,0:T(8,128)(2,1)S(1)}, u32[]{:S(2)}, u32[]{:S(2)}) collective-permute-start(bf16[2,2,2,192,384]{4,3,2,1,0:T(8,128)(2,1)S(1)} %dynamic-slice_bitcast_fusion), channel_id=1, source_target_pairs={{0,2},{2,0},{4,6},{6,4},{8,10},{10,8},{12,14},{14,12},{16,18},{18,... | collective-permute-start | bytes 3538952 | tf_op jit(solution)/shard_map/ppermute | solution.py:56
  314.0 63.0 %collective-permute-start.48 = (bf16[2,2,48,1536]{3,2,1,0:T(8,128)(2,1)S(1)}, bf16[2,2,48,1536]{3,2,1,0:T(8,128)(2,1)S(1)}, u32[]{:S(2)}, u32[]{:S(2)}) collective-permute-start(bf16[2,2,48,1536]{3,2,1,0:T(8,128)(2,1)S(1)} %dynamic-slice_bitcast_fusion.8), channel_id=1, source_target_pairs={{0,2},{2,0},{4,6},{6,4},{8,10},{10,8},{12,14},{14,12},{16,18},{18,... | collective-permute-start | bytes 1769480 | tf_op jit(solution)/shard_map/ppermute | solution.py:56
  316.4 107.8 %collective-permute-start.12 = (bf16[2,2,2,48,1152]{4,3,2,1,0:T(8,128)(2,1)S(1)}, bf16[2,2,2,48,1152]{4,3,2,1,0:T(8,128)(2,1)S(1)}, u32[]{:S(2)}, u32[]{:S(2)}) collective-permute-start(bf16[2,2,2,48,1152]{4,3,2,1,0:T(8,128)(2,1)S(1)} %dynamic-slice_bitcast_fusion.5), channel_id=1, source_target_pairs={{0,8},{2,10},{4,12},{6,14},{8,0},{10,2},{12,4},{14,6},{16,24},{18,... | collective-permute-start | bytes 2654216 | tf_op jit(solution)/shard_map/ppermute | solution.py:56
  320.0 83.8 %collective-permute-start.55 = (bf16[2,2,192,384]{3,2,1,0:T(8,128)(2,1)S(1)}, bf16[2,2,192,384]{3,2,1,0:T(8,128)(2,1)S(1)}, u32[]{:S(2)}, u32[]{:S(2)}) collective-permute-start(bf16[2,2,192,384]{3,2,1,0:T(8,128)(2,1)S(1)} %dynamic-slice_bitcast_fusion.7), channel_id=1, source_target_pairs={{0,2},{2,0},{4,6},{6,4},{8,10},{10,8},{12,14},{14,12},{16,18},{18,... | collective-permute-start | bytes 1769480 | tf_op jit(solution)/shard_map/ppermute | solution.py:56
  377.0 21.7 %collective-permute-start.20 = (bf16[2,2,48,1152]{3,2,1,0:T(8,128)(2,1)S(1)}, bf16[2,2,48,1152]{3,2,1,0:T(8,128)(2,1)S(1)}, u32[]{:S(2)}, u32[]{:S(2)}) collective-permute-start(bf16[2,2,48,1152]{3,2,1,0:T(8,128)(2,1)S(1)} %dynamic-slice_bitcast_fusion.10), channel_id=1, source_target_pairs={{0,2},{2,0},{4,6},{6,4},{8,10},{10,8},{12,14},{14,12},{16,18},{18,... | collective-permute-start | bytes 1327112 | tf_op jit(solution)/shard_map/ppermute | solution.py:56
  402.2 33.8 %collective-permute-start.41 = (bf16[2,2,48,1536]{3,2,1,0:T(8,128)(2,1)S(1)}, bf16[2,2,48,1536]{3,2,1,0:T(8,128)(2,1)S(1)}, u32[]{:S(2)}, u32[]{:S(2)}) collective-permute-start(bf16[2,2,48,1536]{3,2,1,0:T(8,128)(2,1)S(1)} %dynamic-slice_bitcast_fusion.9), channel_id=1, source_target_pairs={{0,4},{2,6},{4,0},{6,2},{8,12},{10,14},{12,8},{14,10},{16,20},{18,... | collective-permute-start | bytes 1769480 | tf_op jit(solution)/shard_map/ppermute | solution.py:56
  403.7 32.5 %collective-permute-start.62 = (bf16[2,2,192,384]{3,2,1,0:T(8,128)(2,1)S(1)}, bf16[2,2,192,384]{3,2,1,0:T(8,128)(2,1)S(1)}, u32[]{:S(2)}, u32[]{:S(2)}) collective-permute-start(bf16[2,2,192,384]{3,2,1,0:T(8,128)(2,1)S(1)} %dynamic-slice_bitcast_fusion.6), channel_id=1, source_target_pairs={{0,4},{2,6},{4,0},{6,2},{8,12},{10,14},{12,8},{14,10},{16,20},{18,... | collective-permute-start | bytes 1769480 | tf_op jit(solution)/shard_map/ppermute | solution.py:56
  407.5 17.5 %collective-permute-start.56 = (bf16[2,192,384]{2,1,0:T(8,128)(2,1)S(1)}, bf16[2,192,384]{2,1,0:T(8,128)(2,1)S(1)}, u32[]{:S(2)}, u32[]{:S(2)}) collective-permute-start(bf16[2,192,384]{2,1,0:T(8,128)(2,1)S(1)} %dynamic-slice_bitcast_fusion.13), channel_id=1, source_target_pairs={{0,8},{2,10},{4,12},{6,14},{8,0},{10,2},{12,4},{14,6},{16,24},{18,... | collective-permute-start | bytes 884744 | tf_op jit(solution)/shard_map/ppermute | solution.py:56
  436.4 18.6 %collective-permute-start.63 = (bf16[2,192,384]{2,1,0:T(8,128)(2,1)S(1)}, bf16[2,192,384]{2,1,0:T(8,128)(2,1)S(1)}, u32[]{:S(2)}, u32[]{:S(2)}) collective-permute-start(bf16[2,192,384]{2,1,0:T(8,128)(2,1)S(1)} %dynamic-slice_bitcast_fusion.12), channel_id=1, source_target_pairs={{0,8},{2,10},{4,12},{6,14},{8,0},{10,2},{12,4},{14,6},{16,24},{18,... | collective-permute-start | bytes 884744 | tf_op jit(solution)/shard_map/ppermute | solution.py:56
  438.7 16.6 %collective-permute-start.14 = (bf16[2,48,1152]{2,1,0:T(8,128)(2,1)S(1)}, bf16[2,48,1152]{2,1,0:T(8,128)(2,1)S(1)}, u32[]{:S(2)}, u32[]{:S(2)}) collective-permute-start(bf16[2,48,1152]{2,1,0:T(8,128)(2,1)S(1)} %dynamic-slice_bitcast_fusion.19), channel_id=1, source_target_pairs={{0,4},{2,6},{4,0},{6,2},{8,12},{10,14},{12,8},{14,10},{16,20},{18,... | collective-permute-start | bytes 663560 | tf_op jit(solution)/shard_map/ppermute | solution.py:56
  (176 other events, 1249.4 us)
